TPU v7x, 32 devices: a whole 2x2x4 slice. The times are simulated.
32 devices in a mesh: groups: 2 (over y), ctx: 8 (over z, x), chan: 2 (over core).
Axes of the slice: x: 2, y: 2, z: 4, core: 2. Of those that a mesh axis runs over, the one named last changes fastest.
Arguments:
- inputs: bfloat16 [2048, 2048], P(('groups', 'ctx'), 'chan'), parts along dimension 0, may hold values from -0.1875 to 0.1875
- out_grad: bfloat16 [2048, 2048], P(('groups', 'ctx'), 'chan'), parts along dimension 0, may hold values from -6 to 6
- filters: bfloat16 [512, 2048], P(None, 'chan'), may hold values from -0.25 to 0.25
Outputs:
- in_grad: bfloat16 [2048, 2048], P(('groups', 'ctx'), 'chan'), parts along dimension 0
- filter_grad: float32 [1024, 2048], P(('groups', 'ctx'), 'chan'), parts along dimension 0
There are 2 independent parts, one for each index of `groups`. A program takes and returns all parts, laid end to end along the dimension named above; an argument that names none is the same for every part. Nothing has to cross between parts.
All inputs are finite; a program needn't handle non-finite values.
Results may differ from a plain program's by a relative error of at most 0.0085.
Values may be sent and summed in bfloat16 or wider, within the bound.
A program may use at most 64 MiB of HBM per device.

v0:
```python
import math

import jax
import jax.numpy as jnp
from jax import lax
from jax.sharding import PartitionSpec as P


def passed_along(value, axis, steps):
    count = lax.axis_size(axis)
    initial, last = (max(0, -steps), min(count, count - steps))
    return lax.ppermute(value, axis, [(source, source + steps) for source in range(initial, last)])


def phase_table(row_ids, col_ids, period):
    return 2.0 * math.pi / period * (row_ids * col_ids % period).astype(jnp.float32)


def split_table(table):
    high_part = table.astype(jnp.bfloat16)
    low_part = (table - high_part.astype(jnp.float32)).astype(jnp.bfloat16)
    return (high_part, low_part)


def forward_apply(parts, data):
    first = jnp.dot(parts[0], data, preferred_element_type=jnp.float32)
    return first + jnp.dot(parts[1], data, preferred_element_type=jnp.float32)


def spectral(table, data):
    return jnp.dot(table, data, precision=lax.Precision.HIGH, preferred_element_type=jnp.float32)


def per_device(inputs, out_grad, filters):
    tok_len = out_grad.shape[0]
    channels = out_grad.shape[1]
    lag_count = filters.shape[0]
    far_reach = lag_count // tok_len
    period = 2 * tok_len
    freq_count = tok_len + 1
    freq_col = jnp.arange(freq_count, dtype=jnp.int32)[:, None]
    time_row = jnp.arange(tok_len, dtype=jnp.int32)[None, :]
    angle_fwd = phase_table(freq_col, time_row, period)
    forward = split_table(jnp.concatenate([jnp.cos(angle_fwd), -jnp.sin(angle_fwd)], axis=0))
    freq_row = jnp.arange(freq_count, dtype=jnp.int32)[None, :]
    weighting = (
        jnp.where((freq_row == 0) | (freq_row == tok_len), 1.0, 2.0).astype(jnp.float32) / period
    )
    back_rows = (tok_len - jnp.arange(tok_len, dtype=jnp.int32))[:, None]
    angle_back = phase_table(back_rows, freq_row, period)
    inverse_in = jnp.concatenate(
        [weighting * jnp.cos(angle_back), -weighting * jnp.sin(angle_back)], axis=1
    )
    lag_rows = ((jnp.arange(period, dtype=jnp.int32) - tok_len) % period)[:, None]
    angle_lag = phase_table(lag_rows, freq_row, period)
    inverse_lag = jnp.concatenate(
        [weighting * jnp.cos(angle_lag), -weighting * jnp.sin(angle_lag)], axis=1
    )
    parity = jnp.where(jnp.arange(freq_count) % 2 == 0, 1.0, -1.0).astype(jnp.float32)
    parity_both = jnp.concatenate([parity, parity])[:, None]
    received = [out_grad]
    current = out_grad
    for offset in range(far_reach):
        current = passed_along(current, "ctx", -1)
        received.append(current)
    tap_blocks = filters.reshape(far_reach, tok_len, channels)
    tap_spec = jnp.einsum("ft,btc->bfc", forward[0], tap_blocks, preferred_element_type=jnp.float32)
    tap_spec = tap_spec + jnp.einsum(
        "ft,btc->bfc", forward[1], tap_blocks, preferred_element_type=jnp.float32
    )
    input_spec = forward_apply(forward, inputs)
    input_re = input_spec[:freq_count]
    input_im = input_spec[freq_count:]
    accum_re = jnp.zeros((freq_count, channels), jnp.float32)
    accum_im = jnp.zeros((freq_count, channels), jnp.float32)
    lag_parts = []
    for offset in range(far_reach + 1):
        grad_spec = forward_apply(forward, received[offset])
        grad_re = grad_spec[:freq_count]
        grad_im = grad_spec[freq_count:]
        if offset >= 1 and offset < far_reach:
            segment = tap_spec[offset - 1] + parity_both * tap_spec[offset]
        elif offset >= 1:
            segment = tap_spec[offset - 1]
        else:
            segment = parity_both * tap_spec[offset]
        seg_re = segment[:freq_count]
        seg_im = segment[freq_count:]
        accum_re = accum_re + grad_re * seg_re + grad_im * seg_im
        accum_im = accum_im + grad_re * seg_im - grad_im * seg_re
        cross = jnp.concatenate(
            [grad_re * input_re + grad_im * input_im, grad_im * input_re - grad_re * input_im],
            axis=0,
        )
        lag_parts.append(spectral(inverse_lag, cross))
    in_grad = spectral(inverse_in, jnp.concatenate([accum_re, accum_im], axis=0)).astype(
        jnp.bfloat16
    )
    segments = [
        lag_parts[index + 1][:tok_len] + lag_parts[index][tok_len:] for index in range(far_reach)
    ]
    partial_value = jnp.concatenate(segments, axis=0)
    filter_grad = lax.psum_scatter(partial_value, "ctx", scatter_dimension=0, tiled=True)
    return (in_grad, filter_grad)


def solution(mesh):
    return jax.shard_map(
        per_device,
        mesh=mesh,
        in_specs=(P(("groups", "ctx"), "chan"), P(("groups", "ctx"), "chan"), P(None, "chan")),
        out_specs=(P(("groups", "ctx"), "chan"), P(("groups", "ctx"), "chan")),
        check_vma=False,
    )
```

profile of v0, /device:TPU:0, one launch (start us, length us, event | category | flops | bytes accessed | tf_op | source)
XLA Modules:
  0.0 131.3 jit_solution(3056980193905968460)
XLA Ops:
  7.2 1.4 %collective-permute-start = (bf16[128,1024]{1,0:T(8,128)(2,1)}, bf16[128,1024]{1,0:T(8,128)(2,1)S(1)}, u32[]{:S(2)}, u32[]{:S(2)}) collective-permute-start(bf16[128,1024]{1,0:T(8,128)(2,1)} %param.4), channel_id=1, source_target_pairs={{2,0},{4,2},{6,4},{8,6},{10,8},{12,10},{14,12},{3,1},{5,3},{7,5},{... | collective-permute-start | bytes 786440 | tf_op jit(solution)/shard_map/ppermute | solution.py:12
  9.0 1.3 fusion.64
  11.9 1.1 cosine_multiply_fusion
  13.0 5.7 %collective-permute-done = bf16[128,1024]{1,0:T(8,128)(2,1)S(1)} collective-permute-done((bf16[128,1024]{1,0:T(8,128)(2,1)}, bf16[128,1024]{1,0:T(8,128)(2,1)S(1)}, u32[]{:S(2)}, u32[]{:S(2)}) %collective-permute-start) | collective-permute-done | bytes 262176 | tf_op jit(solution)/shard_map/ppermute | solution.py:12
  18.8 1.3 collective-permute-start.1
  20.6 8.1 %collective-permute-done.1 = bf16[128,1024]{1,0:T(8,128)(2,1)S(1)} collective-permute-done((bf16[128,1024]{1,0:T(8,128)(2,1)S(1)}, bf16[128,1024]{1,0:T(8,128)(2,1)S(1)}, u32[]{:S(2)}, u32[]{:S(2)}) %collective-permute-start.1) | collective-permute-done | bytes 262176 | tf_op jit(solution)/shard_map/ppermute | solution.py:12
  28.7 1.3 collective-permute-start.2
  31.6 1.1 fusion.12
  32.7 5.1 %collective-permute-done.2 = bf16[128,1024]{1,0:T(8,128)(2,1)S(1)} collective-permute-done((bf16[128,1024]{1,0:T(8,128)(2,1)S(1)}, bf16[128,1024]{1,0:T(8,128)(2,1)S(1)}, u32[]{:S(2)}, u32[]{:S(2)}) %collective-permute-start.2) | collective-permute-done | bytes 262176 | tf_op jit(solution)/shard_map/ppermute | solution.py:12
  39.4 1.1 fusion.16
  40.5 1.1 fusion.5
  41.6 1.5 %collective-permute-start.3 = (bf16[128,1024]{1,0:T(8,128)(2,1)S(1)}, bf16[128,1024]{1,0:T(8,128)(2,1)S(1)}, u32[]{:S(2)}, u32[]{:S(2)}) collective-permute-start(bf16[128,1024]{1,0:T(8,128)(2,1)S(1)} %collective-permute-done.2), channel_id=1, source_target_pairs={{2,0},{4,2},{6,4},{8,6},{10,8},{12,10},{14,12},{3,1},{5,3},{7,5},{... | collective-permute-start | bytes 786440 | tf_op jit(solution)/shard_map/ppermute | solution.py:12
  43.2 0.7 convolution_add_fusion.7
  43.9 6.6 %collective-permute-done.3 = bf16[128,1024]{1,0:T(8,128)(2,1)S(1)} collective-permute-done((bf16[128,1024]{1,0:T(8,128)(2,1)S(1)}, bf16[128,1024]{1,0:T(8,128)(2,1)S(1)}, u32[]{:S(2)}, u32[]{:S(2)}) %collective-permute-start.3) | collective-permute-done | bytes 262176 | tf_op jit(solution)/shard_map/ppermute | solution.py:12
  51.4 0.7 copy-done.5
  52.1 0.7 convolution_add_fusion.6
  52.8 1.5 %pad_maximum_fusion = f32[512,1024]{1,0:T(8,128)} fusion(f32[128,1024]{1,0:T(8,128)S(1)} %convolution_add_fusion.6, f32[128,1024]{1,0:T(8,128)S(1)} %get-tuple-element.23, f32[128,1024]{1,0:T(8,128)S(1)} %get-tuple-element.22, f32[128,1024]{1,0:T(8,128)S(1)} %convolution_add_fusion.7), kind=kLoop, calls=%fused_computation.1 | loop fusion | flops 1572864 | bytes 4194304 | tf_op jit(solution)/shard_map/concatenate | solution.py:102
  55.0 0.7 fusion.51
  55.8 0.7 add_bitcast_fusion
  56.6 1.0 fusion.23
  58.4 1.4 %multiply_subtract_fusion.5 = f32[129,1024]{1,0:T(8,128)S(1)} fusion(f32[4,258,1024]{2,1,0:T(8,128)S(1)} %add_bitcast_fusion, f32[258,1024]{1,0:T(8,128)S(1)} %get-tuple-element.5, f32[258,1024]{1,0:T(8,128)S(1)} %get-tuple-element.7, f32[258,1024]{1,0:T(8,128)S(1)} %get-tuple-element.6, f32[258,1024]{1,0:T(8,128)S(1)} %get-tuple-element.4, ...), kind=kLoop, calls=%fused_computation.53 | loop fusion | flops 2509824 | bytes 11096064 | tf_op jit(solution)/shard_map/sub | solution.py:90
  59.8 1.4 %multiply_add_fusion.7 = f32[129,1024]{1,0:T(8,128)S(1)} fusion(f32[4,258,1024]{2,1,0:T(8,128)S(1)} %add_bitcast_fusion, f32[258,1024]{1,0:T(8,128)S(1)} %get-tuple-element.5, f32[258,1024]{1,0:T(8,128)S(1)} %get-tuple-element.7, f32[258,1024]{1,0:T(8,128)S(1)} %get-tuple-element.6, f32[258,1024]{1,0:T(8,128)S(1)} %get-tuple-element.4, ...), kind=kLoop, calls=%fused_computation.54 | loop fusion | flops 2509824 | bytes 11096064 | tf_op jit(solution)/shard_map/add | solution.py:89
  61.1 1.4 %convolution_convert_fusion = bf16[128,1024]{1,0:T(8,128)(2,1)} fusion(f32[129,1024]{1,0:T(8,128)S(1)} %multiply_subtract_fusion.5, f32[129,1024]{1,0:T(8,128)S(1)} %multiply_add_fusion.7, f32[128,129]{1,0:T(8,128)S(1)} %get-tuple-element.27, f32[128,129]{1,0:T(8,128)S(1)} %get-tuple-element.26), kind=kOutput, calls=%fused_computation.10 | convolution fusion | flops 203327744 | bytes 1451008 | tf_op jit(solution)/shard_map/dot_general | solution.py:31
  62.5 62.0 %reduce-scatter.2.cloned.1.call-done = f32[64,1024]{1,0:T(8,128)} async-done(((f32[512,1024]{1,0:T(8,128)}), f32[64,1024]{1,0:T(8,128)}) %reduce-scatter.2.cloned.1.call-update) | async-done | bytes 262160 | tf_op jit(solution)/shard_map/reduce_scatter | solution.py:103
  (44 shorter events, 8.1 us)
Async XLA Ops:
  7.2 47.9 %copy-start = (bf16[512,1024]{1,0:T(8,128)(2,1)S(1)}, bf16[512,1024]{1,0:T(8,128)(2,1)}, u32[]{:S(2)}) copy-start(bf16[512,1024]{1,0:T(8,128)(2,1)} %param.5) | copy-start | bytes 3145732
  7.2 3.1 %copy-start.7 = (bf16[128,1024]{1,0:T(8,128)(2,1)S(1)}, bf16[128,1024]{1,0:T(8,128)(2,1)}, u32[]{:S(2)}) copy-start(bf16[128,1024]{1,0:T(8,128)(2,1)} %param.3) | copy-start | bytes 786436
  7.2 117.3 %reduce-scatter.2.cloned.1.call-start = ((), (), s32[]{:S(2)}) async-start(), calls=%async_computation.1 | async-start | bytes 2359296 | tf_op jit(solution)/shard_map/reduce_scatter | solution.py:103
  7.2 11.5 %collective-permute-start = (bf16[128,1024]{1,0:T(8,128)(2,1)}, bf16[128,1024]{1,0:T(8,128)(2,1)S(1)}, u32[]{:S(2)}, u32[]{:S(2)}) collective-permute-start(bf16[128,1024]{1,0:T(8,128)(2,1)} %param.4), channel_id=1, source_target_pairs={{2,0},{4,2},{6,4},{8,6},{10,8},{12,10},{14,12},{3,1},{5,3},{7,5},{... | collective-permute-start | bytes 786440 | tf_op jit(solution)/shard_map/ppermute | solution.py:12
  9.0 1.6 %copy-start.9 = (bf16[128,1024]{1,0:T(8,128)(2,1)S(1)}, bf16[128,1024]{1,0:T(8,128)(2,1)}, u32[]{:S(2)}) copy-start(bf16[128,1024]{1,0:T(8,128)(2,1)} %param.4) | copy-start | bytes 786436
  10.6 1.0 copy-start.8
  18.8 10.0 %collective-permute-start.1 = (bf16[128,1024]{1,0:T(8,128)(2,1)S(1)}, bf16[128,1024]{1,0:T(8,128)(2,1)S(1)}, u32[]{:S(2)}, u32[]{:S(2)}) collective-permute-start(bf16[128,1024]{1,0:T(8,128)(2,1)S(1)} %collective-permute-done), channel_id=1, source_target_pairs={{2,0},{4,2},{6,4},{8,6},{10,8},{12,10},{14,12},{3,1},{5,3},{7,5},{... | collective-permute-start | bytes 786440 | tf_op jit(solution)/shard_map/ppermute | solution.py:12
  28.7 9.1 %collective-permute-start.2 = (bf16[128,1024]{1,0:T(8,128)(2,1)S(1)}, bf16[128,1024]{1,0:T(8,128)(2,1)S(1)}, u32[]{:S(2)}, u32[]{:S(2)}) collective-permute-start(bf16[128,1024]{1,0:T(8,128)(2,1)S(1)} %collective-permute-done.1), channel_id=1, source_target_pairs={{2,0},{4,2},{6,4},{8,6},{10,8},{12,10},{14,12},{3,1},{5,3},{7,5},{... | collective-permute-start | bytes 786440 | tf_op jit(solution)/shard_map/ppermute | solution.py:12
  30.6 1.0 copy-start.1
  38.4 1.0 copy-start.3
  41.6 8.9 %collective-permute-start.3 = (bf16[128,1024]{1,0:T(8,128)(2,1)S(1)}, bf16[128,1024]{1,0:T(8,128)(2,1)S(1)}, u32[]{:S(2)}, u32[]{:S(2)}) collective-permute-start(bf16[128,1024]{1,0:T(8,128)(2,1)S(1)} %collective-permute-done.2), channel_id=1, source_target_pairs={{2,0},{4,2},{6,4},{8,6},{10,8},{12,10},{14,12},{3,1},{5,3},{7,5},{... | collective-permute-start | bytes 786440 | tf_op jit(solution)/shard_map/ppermute | solution.py:12
  51.1 1.0 copy-start.5
  56.5 1.2 copy-start.2
  56.5 1.6 %copy-start.4 = (f32[258,1024]{1,0:T(8,128)S(1)}, f32[258,1024]{1,0:T(8,128)}, u32[]{:S(2)}) copy-start(f32[258,1024]{1,0:T(8,128)} %copy-done.3) | copy-start | bytes 3170308
  56.5 1.9 %copy-start.6 = (f32[258,1024]{1,0:T(8,128)S(1)}, f32[258,1024]{1,0:T(8,128)}, u32[]{:S(2)}) copy-start(f32[258,1024]{1,0:T(8,128)} %copy-done.5) | copy-start | bytes 3170308
Sparse Core Ops, SparseCore 0:
  54.5 69.9 reduce-scatter.1
where the time goes:
time: 132 us; the launch traced here: 131 us
  waiting for transfers between devices  87.5 us (66%)
  between operations  14.4 us (11%)
  matrix products  11.9 us (9%)
  other arithmetic  8.8 us (7%)
  starting transfers between devices  5.49 us (4%)
  local copies, waits for them, and re-layouts  3.23 us (2%)
    reduce_scatter x1, waiting for transfers between devices, per_device(): lax.psum_scatter(partial_value, 'ctx', scatter_dimension=0, tiled=True)  62 us
    ppermute x4, waiting for transfers between devices, passed_along(): lax.ppermute(value, axis, [(source, source + steps) for source in range(i...  25.5 us
    dot_general x6, matrix products, spectral(): jnp.dot(table, data, precision=lax.Precision.HIGH, preferred_element_type...  5.95 us
    ppermute x4, starting transfers between devices, passed_along(): lax.ppermute(value, axis, [(source, source + steps) for source in range(i...  5.46 us
    unnamed x20, local copies, waits for them, and re-layouts  3.23 us
    dot_general x6, matrix products, forward_apply(): first = jnp.dot(parts[0], data, preferred_element_type=jnp.float32)  2.75 us
  transfers between devices with their start and end apart: 5, of which 5 were waited for; matrix products, arithmetic and copies ran while one was open for 11% of the time, Pallas kernels for 0%

commit v1 on v0

--- a/solution.py
+++ b/solution.py
@@ -1,9 +1,16 @@
+import functools
 import math
 
 import jax
 import jax.numpy as jnp
+import numpy as np
 from jax import lax
+from jax.experimental import pallas as pl
+from jax.experimental.pallas import tpu as pltpu
 from jax.sharding import PartitionSpec as P
+
+LANES = 128
+CHUNK = 16
 
 
 def passed_along(value, axis, steps):
@@ -31,7 +38,7 @@
     return jnp.dot(table, data, precision=lax.Precision.HIGH, preferred_element_type=jnp.float32)
 
 
-def per_device(inputs, out_grad, filters):
+def general_plan(inputs, out_grad, filters):
     tok_len = out_grad.shape[0]
     channels = out_grad.shape[1]
     lag_count = filters.shape[0]
@@ -104,6 +111,265 @@
     return (in_grad, filter_grad)
 
 
+def table_parts(table):
+    high_part = table.astype(jnp.bfloat16)
+    low_part = (table - high_part.astype(np.float64)).astype(jnp.bfloat16)
+    return np.stack([high_part, low_part])
+
+
+def transform_tables(block):
+    order = np.concatenate([np.arange(0, block, 2), np.arange(1, block, 2)])
+    steps = (2 * order + 1)[:, None] * np.arange(block)[None, :] % (4 * block)
+    angle = np.pi / (2 * block) * steps
+    forward = np.concatenate([np.cos(angle), np.sin(angle)], axis=0)
+    return table_parts(forward), table_parts(forward.T / block)
+
+
+def peer_order(count):
+    return sorted(range(1, count), key=lambda step: (abs(2 * step - count), step))
+
+
+def exchange_kernel(
+    count, block,
+    in_ref, grad_ref, taps_ref, fwd_hbm, inv_hbm,
+    out_ref, lag_ref,
+    u_buf, g_buf, tap_buf, fwd, inv, g_spec, u_spec, tap_spec, seg_spec, r_high, r_low, q_high, q_low,
+    out_buf, lag_buf, send_sem, recv_sem, local_sem,
+):
+    me = lax.axis_index("ctx")
+    tok_len = in_ref.shape[0]
+    width = g_buf.shape[2]
+    lag_count = taps_ref.shape[0]
+    own_lags = lag_count // count
+    per_block = block // tok_len
+    blocks = g_buf.shape[0]
+    segs = lag_count // block
+    order = peer_order(count)
+
+    def cols(index):
+        return pl.ds(pl.multiple_of(index * width, LANES), width)
+
+    def place(buf, index):
+        rows = pl.ds(pl.multiple_of(lax.rem(index, per_block) * tok_len, tok_len), tok_len)
+        return buf.at[lax.div(index, per_block), rows, :]
+
+    my_cols = cols(me)
+    local = [
+        pltpu.make_async_copy(fwd_hbm, fwd, local_sem.at[0]),
+        pltpu.make_async_copy(taps_ref.at[:, my_cols], tap_buf, local_sem.at[1]),
+        pltpu.make_async_copy(grad_ref.at[:, my_cols], place(g_buf, me), local_sem.at[2]),
+        pltpu.make_async_copy(in_ref.at[:, my_cols], place(u_buf, me), local_sem.at[3]),
+        pltpu.make_async_copy(inv_hbm, inv, local_sem.at[4]),
+    ]
+    barrier = pltpu.get_barrier_semaphore()
+    for step in order:
+        pl.semaphore_signal(
+            barrier, inc=1, device_id={"ctx": lax.rem(me + step, count)},
+            device_id_type=pl.DeviceIdType.MESH,
+        )
+    for copy in local:
+        copy.start()
+    pl.semaphore_wait(barrier, count - 1)
+
+    def send_all(kind, source, target):
+        copies = []
+        for step in order:
+            peer = lax.rem(me + step, count)
+            copies.append(
+                pltpu.make_async_remote_copy(
+                    src_ref=source(peer),
+                    dst_ref=target,
+                    send_sem=send_sem.at[kind, step],
+                    recv_sem=recv_sem.at[kind, step],
+                    device_id={"ctx": peer},
+                    device_id_type=pl.DeviceIdType.MESH,
+                )
+            )
+            copies[-1].start()
+        return copies
+
+    g_copies = send_all(0, lambda peer: grad_ref.at[:, cols(peer)], place(g_buf, me))
+    u_copies = send_all(1, lambda peer: in_ref.at[:, cols(peer)], place(u_buf, me))
+
+    def forward(data):
+        first = jnp.dot(fwd[0], data, preferred_element_type=jnp.float32)
+        return first + jnp.dot(fwd[1], data, preferred_element_type=jnp.float32)
+
+    def inverse(high, low):
+        first = jnp.dot(inv[0], high, preferred_element_type=jnp.float32)
+        second = jnp.dot(inv[1], high, preferred_element_type=jnp.float32)
+        return first + (second + jnp.dot(inv[0], low, preferred_element_type=jnp.float32))
+
+    def lanes(index):
+        return slice(index * width, (index + 1) * width)
+
+    def over_chunks(body):
+        half = block // 2 // CHUNK
+        for sign, start in ((1.0, 0), (-1.0, half)):
+            def step(index, carry, sign=sign):
+                row = pl.multiple_of(index * CHUNK, CHUNK)
+                body(pl.ds(row, CHUNK), pl.ds(row + block, CHUNK), sign)
+                return carry
+            lax.fori_loop(start, start + half, step, 0)
+
+    def store_split(high, low, rows, where, value):
+        top = value.astype(jnp.bfloat16)
+        high[rows, where] = top
+        low[rows, where] = (value - top.astype(jnp.float32)).astype(jnp.bfloat16)
+
+    local[0].wait()
+    local[1].wait()
+    tap_spec[...] = forward(
+        jnp.concatenate([tap_buf[s * block:(s + 1) * block, :] for s in range(segs)], axis=1)
+    )
+
+    def segment_chunk(re, im, sign):
+        for d in range(segs + 1):
+            real = imag = 0.0
+            if d < segs:
+                real, imag = tap_spec[re, lanes(d)], tap_spec[im, lanes(d)]
+            if d > 0:
+                real = real + sign * tap_spec[im, lanes(d - 1)]
+                imag = imag - sign * tap_spec[re, lanes(d - 1)]
+            seg_spec[re, lanes(d)] = real
+            seg_spec[im, lanes(d)] = imag
+
+    over_chunks(segment_chunk)
+
+    local[2].wait()
+    for copy in g_copies:
+        copy.wait_recv()
+    g_spec[...] = forward(jnp.concatenate([g_buf[b] for b in range(blocks)], axis=1))
+
+    def in_chunk(re, im, sign):
+        grads = [(g_spec[re, lanes(b)], g_spec[im, lanes(b)]) for b in range(blocks)]
+        taps = [(seg_spec[re, lanes(d)], seg_spec[im, lanes(d)]) for d in range(segs + 1)]
+        for b in range(blocks):
+            real = imag = 0.0
+            for d in range(min(segs + 1, blocks - b)):
+                gr, gi = grads[b + d]
+                hr, hi = taps[d]
+                real = real + (gr * hr + gi * hi)
+                imag = imag + (gi * hr - gr * hi)
+            store_split(r_high, r_low, re, lanes(b), real)
+            store_split(r_high, r_low, im, lanes(b), imag)
+
+    over_chunks(in_chunk)
+    local[4].wait()
+    result = inverse(r_high[...], r_low[...]).astype(jnp.bfloat16)
+    for index in range(count):
+        rows = index % per_block * tok_len
+        out_buf[index] = result[rows:rows + tok_len, lanes(index // per_block)]
+    out_copies = send_all(2, lambda peer: out_buf.at[peer], out_ref.at[:, my_cols])
+    own_out = pltpu.make_async_copy(out_buf.at[me], out_ref.at[:, my_cols], local_sem.at[5])
+    own_out.start()
+
+    local[3].wait()
+    for copy in u_copies:
+        copy.wait_recv()
+    u_spec[...] = forward(jnp.concatenate([u_buf[b] for b in range(blocks)], axis=1))
+
+    def lag_chunk(re, im, sign):
+        grads = [(g_spec[re, lanes(b)], g_spec[im, lanes(b)]) for b in range(blocks)]
+        values = [(u_spec[re, lanes(b)], u_spec[im, lanes(b)]) for b in range(blocks)]
+        cross = []
+        for d in range(segs + 1):
+            real = imag = jnp.zeros((CHUNK, width), jnp.float32)
+            for b in range(d, blocks):
+                gr, gi = grads[b]
+                ur, ui = values[b - d]
+                real = real + (gr * ur + gi * ui)
+                imag = imag + (gi * ur - gr * ui)
+            cross.append((real, imag))
+        for s in range(segs):
+            store_split(q_high, q_low, re, lanes(s), cross[s][0] - sign * cross[s + 1][1])
+            store_split(q_high, q_low, im, lanes(s), cross[s][1] + sign * cross[s + 1][0])
+
+    over_chunks(lag_chunk)
+    lag_result = inverse(q_high[...], q_low[...]).astype(jnp.bfloat16)
+    for index in range(count):
+        rows = index * own_lags % block
+        lag_buf[index] = lag_result[rows:rows + own_lags, lanes(index * own_lags // block)]
+    lag_copies = send_all(3, lambda peer: lag_buf.at[peer], lag_ref.at[:, my_cols])
+    own_lag = pltpu.make_async_copy(lag_buf.at[me], lag_ref.at[:, my_cols], local_sem.at[6])
+    own_lag.start()
+
+    for copy in g_copies + u_copies:
+        copy.wait_send()
+    own_out.wait()
+    own_lag.wait()
+    for copy in out_copies + lag_copies:
+        copy.wait()
+
+
+def block_length(tok_len, count, lag_count):
+    block = tok_len
+    if count % 2 == 0 and lag_count % (2 * tok_len) == 0:
+        block = 2 * tok_len
+    return block
+
+
+def whole_lanes(tok_len, channels, lag_count, count):
+    block = block_length(tok_len, count, lag_count)
+    return (
+        count > 1
+        and channels % (count * LANES) == 0
+        and tok_len % CHUNK == 0
+        and block % (2 * CHUNK) == 0
+        and lag_count % block == 0
+        and lag_count % (count * CHUNK) == 0
+        and block % (lag_count // count) == 0
+        and count * tok_len <= 4 * lag_count
+    )
+
+
+def per_device(inputs, out_grad, filters):
+    tok_len, channels = out_grad.shape
+    lag_count = filters.shape[0]
+    count = lax.axis_size("ctx")
+    if not whole_lanes(tok_len, channels, lag_count, count):
+        return general_plan(inputs, out_grad, filters)
+    block = block_length(tok_len, count, lag_count)
+    width = channels // count
+    blocks = count * tok_len // block
+    segs = lag_count // block
+    own_lags = lag_count // count
+    fwd, inv = transform_tables(block)
+    bf16, f32 = jnp.bfloat16, jnp.float32
+    anywhere = pl.BlockSpec(memory_space=pl.ANY)
+    in_grad, lag_grad = pl.pallas_call(
+        functools.partial(exchange_kernel, count, block),
+        out_shape=(
+            jax.ShapeDtypeStruct((tok_len, channels), bf16),
+            jax.ShapeDtypeStruct((own_lags, channels), bf16),
+        ),
+        in_specs=[anywhere] * 5,
+        out_specs=(anywhere, anywhere),
+        scratch_shapes=[
+            pltpu.VMEM((blocks, block, width), bf16),
+            pltpu.VMEM((blocks, block, width), bf16),
+            pltpu.VMEM((lag_count, width), bf16),
+            pltpu.VMEM(fwd.shape, bf16),
+            pltpu.VMEM(inv.shape, bf16),
+            pltpu.VMEM((2 * block, blocks * width), f32),
+            pltpu.VMEM((2 * block, blocks * width), f32),
+            pltpu.VMEM((2 * block, segs * width), f32),
+            pltpu.VMEM((2 * block, (segs + 1) * width), f32),
+            pltpu.VMEM((2 * block, blocks * width), bf16),
+            pltpu.VMEM((2 * block, blocks * width), bf16),
+            pltpu.VMEM((2 * block, segs * width), bf16),
+            pltpu.VMEM((2 * block, segs * width), bf16),
+            pltpu.VMEM((count, tok_len, width), bf16),
+            pltpu.VMEM((count, own_lags, width), bf16),
+            pltpu.SemaphoreType.DMA((4, count)),
+            pltpu.SemaphoreType.DMA((4, count)),
+            pltpu.SemaphoreType.DMA((7,)),
+        ],
+        compiler_params=pltpu.CompilerParams(collective_id=0, has_side_effects=True),
+    )(inputs, out_grad, filters, jnp.asarray(fwd), jnp.asarray(inv))
+    return in_grad, lag_grad.astype(f32)
+
+
 def solution(mesh):
     return jax.shard_map(
         per_device,

time: 132 us -> 33.2 us (0.25)
  waiting for transfers between devices: 87.5 us -> 0 us
  Pallas kernels: 0 us -> 30 us
  between operations: 14.4 us -> 0.65 us
  matrix products: 11.9 us -> 0 us
  other arithmetic: 8.8 us -> 1.67 us
  starting transfers between devices: 5.49 us -> 0 us
  local copies, waits for them, and re-layouts: 3.23 us -> 0.71 us
    reduce_scatter x1 -> x0, waiting for transfers between devices: 62 us -> none  [per_device(): lax.psum_scatter(partial_value, 'ctx', scatter_dimension=0, tiled=True)]
    pallas_call x0 -> x1, Pallas kernels: none -> 30 us  [per_device(): pl.pallas_call(functools.partial(exchange_kernel, count, block), out_shap...]
    ppermute x4 -> x0, waiting for transfers between devices: 25.5 us -> none  [passed_along(): lax.ppermute(value, axis, [(source, source + steps) for source in range(i...]
    dot_general x20 -> x0, matrix products: 11.9 us -> none  [the longest x6 5.95 us: spectral(): jnp.dot(table, data, precision=lax.Precision.HIGH, preferred_element_type...]
    ppermute x4 -> x0, starting transfers between devices: 5.46 us -> none  [passed_along(): lax.ppermute(value, axis, [(source, source + steps) for source in range(i...]
    mul x3 -> x0, other arithmetic: 2.76 us -> none  [the longest x1 1.12 us: per_device(): weighting * jnp.cos(angle_lag)]
    add x5 -> x0, other arithmetic: 2.75 us -> none  [the longest x1 1.36 us: per_device(): accum_re = accum_re + grad_re * seg_re + grad_im * seg_im]
    unnamed x20 -> x3, local copies, waits for them, and re-layouts: 3.23 us -> 0.71 us
  transfers between devices with their start and end apart: 5 -> 0, of which waited for: 5 -> 0; matrix products, arithmetic and copies ran while one was open for 11% -> 0% of each run, Pallas kernels for 0% -> 0%
where the time goes in v1:
time: 33.2 us; the launch traced here: 33 us
  Pallas kernels  30 us (90%)
  other arithmetic  1.67 us (5%)
  local copies, waits for them, and re-layouts  0.71 us (2%)
  between operations  0.65 us (2%)
    pallas_call x1, Pallas kernels, per_device(): pl.pallas_call(functools.partial(exchange_kernel, count, block), out_shap...  30 us
    convert_element_type x1, other arithmetic, per_device(): return (in_grad, lag_grad.astype(f32))  1.67 us
    unnamed x3, local copies, waits for them, and re-layouts  0.71 us

profile of v1, /device:TPU:0, one launch (start us, length us, event | category | flops | bytes accessed | tf_op | source)
XLA Modules:
  0.0 33.0 jit_solution(1412979328481116543)
XLA Ops:
  0.6 30.0 %shard_map.68 = (bf16[128,1024]{1,0:T(8,128)(2,1)}, bf16[64,1024]{1,0:T(8,128)(2,1)}) custom-call(bf16[128,1024]{1,0:T(8,128)(2,1)} %in_ref.1, bf16[128,1024]{1,0:T(8,128)(2,1)} %grad_ref.1, bf16[512,1024]{1,0:T(8,128)(2,1)} %taps_ref.1, bf16[2,512,256]{2,1,0:T(8,128)(2,1)} %constant.4.clone.fwd_hbm, bf16[2,256,512]{2,1,0:T(8,128)(2,1)} %constant.5.clone.inv_hbm), custom_call_target="tpu_custom_call" | custom-call | tf_op jit(solution)/shard_map/pallas_call | solution.py:340
  30.6 0.0 copy-start
  30.6 1.7 %convert_element_type.3 = f32[64,1024]{1,0:T(8,128)} convert(bf16[64,1024]{1,0:T(8,128)(2,1)} %get-tuple-element.5) | non-fusion elementwise | flops 65536 | bytes 393216 | tf_op jit(solution)/shard_map/convert_element_type | solution.py:370
  32.3 0.0 copy-done
  32.3 0.7 %copy.8 = bf16[128,1024]{1,0:T(8,128)(2,1)} copy(bf16[128,1024]{1,0:T(8,128)(2,1)S(1)} %copy-done) | data formatting | bytes 524288
Async XLA Ops:
  30.6 1.7 %copy-start = (bf16[128,1024]{1,0:T(8,128)(2,1)S(1)}, bf16[128,1024]{1,0:T(8,128)(2,1)}, u32[]{:S(2)}) copy-start(bf16[128,1024]{1,0:T(8,128)(2,1)} %get-tuple-element.8) | copy-start | bytes 786436

commit v2 on v1

--- a/solution.py
+++ b/solution.py
@@ -126,7 +126,7 @@
 
 
 def peer_order(count):
-    return sorted(range(1, count), key=lambda step: (abs(2 * step - count), step))
+    return sorted(range(1, count), key=lambda step: (-abs(2 * step - count), step))
 
 
 def exchange_kernel(
@@ -302,6 +302,16 @@
         copy.wait()
 
 
+def finish_kernel(in_ref, lag_ref, in_out, lag_out, lag_wide, sem):
+    move = pltpu.make_async_copy(in_ref, in_out, sem.at[0])
+    move.start()
+    lag_wide[...] = lag_ref[...].astype(lag_wide.dtype)
+    store = pltpu.make_async_copy(lag_wide, lag_out, sem.at[1])
+    store.start()
+    move.wait()
+    store.wait()
+
+
 def block_length(tok_len, count, lag_count):
     block = tok_len
     if count % 2 == 0 and lag_count % (2 * tok_len) == 0:
@@ -337,14 +347,15 @@
     fwd, inv = transform_tables(block)
     bf16, f32 = jnp.bfloat16, jnp.float32
     anywhere = pl.BlockSpec(memory_space=pl.ANY)
+    in_vmem = pl.BlockSpec(memory_space=pltpu.VMEM)
     in_grad, lag_grad = pl.pallas_call(
         functools.partial(exchange_kernel, count, block),
         out_shape=(
-            jax.ShapeDtypeStruct((tok_len, channels), bf16),
-            jax.ShapeDtypeStruct((own_lags, channels), bf16),
+            pltpu.VMEM((tok_len, channels), bf16),
+            pltpu.VMEM((own_lags, channels), bf16),
         ),
         in_specs=[anywhere] * 5,
-        out_specs=(anywhere, anywhere),
+        out_specs=(in_vmem, in_vmem),
         scratch_shapes=[
             pltpu.VMEM((blocks, block, width), bf16),
             pltpu.VMEM((blocks, block, width), bf16),
@@ -367,7 +378,22 @@
         ],
         compiler_params=pltpu.CompilerParams(collective_id=0, has_side_effects=True),
     )(inputs, out_grad, filters, jnp.asarray(fwd), jnp.asarray(inv))
-    return in_grad, lag_grad.astype(f32)
+    return pl.pallas_call(
+        finish_kernel,
+        out_shape=(
+            jax.ShapeDtypeStruct(in_grad.shape, bf16),
+            jax.ShapeDtypeStruct(lag_grad.shape, f32),
+        ),
+        in_specs=[in_vmem, in_vmem],
+        out_specs=(anywhere, anywhere),
+        scratch_shapes=[
+            pltpu.VMEM(lag_grad.shape, f32),
+            pltpu.SemaphoreType.DMA((2,)),
+        ],
+    )(
+        pltpu.with_memory_space_constraint(in_grad, pltpu.VMEM),
+        pltpu.with_memory_space_constraint(lag_grad, pltpu.VMEM),
+    )
 
 
 def solution(mesh):

time: 33.2 us -> 29.1 us (0.88)
  other arithmetic: 1.67 us -> 0 us
  Pallas kernels: 30 us -> 28.4 us
  local copies, waits for them, and re-layouts: 0.71 us -> 0 us
    pallas_call x1, Pallas kernels: 30 us -> 27.6 us  [per_device(): pl.pallas_call(functools.partial(exchange_kernel, count, block), out_shap...]
    convert_element_type x1 -> x0, other arithmetic: 1.67 us -> none  [per_device(): return (in_grad, lag_grad.astype(f32))]
    pallas_call x0 -> x1, Pallas kernels: none -> 0.81 us  [per_device(): pl.pallas_call(finish_kernel, out_shape=(jax.ShapeDtypeStruct(in_grad.sha...]
    unnamed x3 -> x0, local copies, waits for them, and re-layouts: 0.71 us -> none
where the time goes in v2:
time: 29.1 us; the launch traced here: 29 us
  Pallas kernels  28.4 us (98%)
  between operations  0.64 us (2%)
    pallas_call x1, Pallas kernels, per_device(): pl.pallas_call(functools.partial(exchange_kernel, count, block), out_shap...  27.6 us
    pallas_call x1, Pallas kernels, per_device(): pl.pallas_call(finish_kernel, out_shape=(jax.ShapeDtypeStruct(in_grad.sha...  0.81 us

profile of v2, /device:TPU:0, one launch (start us, length us, event | category | flops | bytes accessed | tf_op | source)
XLA Modules:
  0.0 29.0 jit_solution(17637549192341535196)
XLA Ops:
  0.6 27.6 %shard_map.68 = (bf16[128,1024]{1,0:T(8,128)(2,1)S(1)}, bf16[64,1024]{1,0:T(8,128)(2,1)S(1)}) custom-call(bf16[128,1024]{1,0:T(8,128)(2,1)} %in_ref.1, bf16[128,1024]{1,0:T(8,128)(2,1)} %grad_ref.1, bf16[512,1024]{1,0:T(8,128)(2,1)} %taps_ref.1, bf16[2,512,256]{2,1,0:T(8,128)(2,1)} %constant.4.clone.fwd_hbm, bf16[2,256,512]{2,1,0:T(8,128)(2,1)} %constant.5.clone.inv_hbm), custom_call_target="tpu_custom_call" | custom-call | tf_op jit(solution)/shard_map/pallas_call | solution.py:351
  28.2 0.8 %shard_map.69 = (bf16[128,1024]{1,0:T(8,128)(2,1)}, f32[64,1024]{1,0:T(8,128)}) custom-call(bf16[128,1024]{1,0:T(8,128)(2,1)S(1)} %get-tuple-element.4.in_ref, bf16[64,1024]{1,0:T(8,128)(2,1)S(1)} %get-tuple-element.5.lag_ref), custom_call_target="tpu_custom_call" | custom-call | tf_op jit(solution)/shard_map/pallas_call | solution.py:381

commit v3 on v2

--- a/solution.py
+++ b/solution.py
@@ -173,7 +173,7 @@
 
     def send_all(kind, source, target):
         copies = []
-        for step in order:
+        for step in order if kind % 2 == 0 else order[::-1]:
             peer = lax.rem(me + step, count)
             copies.append(
                 pltpu.make_async_remote_copy(

time: 29.1 us -> 29 us (level)
  no operation moved by 1% of the time
where the time goes in v3:
time: 29 us; the launch traced here: 28.8 us
  Pallas kernels  28.2 us (97%)
  between operations  0.64 us (2%)
    pallas_call x1, Pallas kernels, per_device(): pl.pallas_call(functools.partial(exchange_kernel, count, block), out_shap...  27.4 us
    pallas_call x1, Pallas kernels, per_device(): pl.pallas_call(finish_kernel, out_shape=(jax.ShapeDtypeStruct(in_grad.sha...  0.81 us

profile of v3, /device:TPU:0, one launch (start us, length us, event | category | flops | bytes accessed | tf_op | source)
XLA Modules:
  0.0 28.8 jit_solution(10647690896096254705)
XLA Ops:
  0.6 27.4 %shard_map.68 = (bf16[128,1024]{1,0:T(8,128)(2,1)S(1)}, bf16[64,1024]{1,0:T(8,128)(2,1)S(1)}) custom-call(bf16[128,1024]{1,0:T(8,128)(2,1)} %in_ref.1, bf16[128,1024]{1,0:T(8,128)(2,1)} %grad_ref.1, bf16[512,1024]{1,0:T(8,128)(2,1)} %taps_ref.1, bf16[2,512,256]{2,1,0:T(8,128)(2,1)} %constant.4.clone.fwd_hbm, bf16[2,256,512]{2,1,0:T(8,128)(2,1)} %constant.5.clone.inv_hbm), custom_call_target="tpu_custom_call" | custom-call | tf_op jit(solution)/shard_map/pallas_call | solution.py:351
  28.0 0.8 %shard_map.69 = (bf16[128,1024]{1,0:T(8,128)(2,1)}, f32[64,1024]{1,0:T(8,128)}) custom-call(bf16[128,1024]{1,0:T(8,128)(2,1)S(1)} %get-tuple-element.4.in_ref, bf16[64,1024]{1,0:T(8,128)(2,1)S(1)} %get-tuple-element.5.lag_ref), custom_call_target="tpu_custom_call" | custom-call | tf_op jit(solution)/shard_map/pallas_call | solution.py:381
